TPU v7x, 256 devices: a whole 4x4x8 slice. The times are simulated.
256 devices in a mesh: clique: 8 (over y_hi, x), copy: 32 (over z, y_lo, core).
Axes of the slice: x: 4, y: 4 (y_hi: 2, y_lo: 2; y = y_hi * 2 + y_lo), z: 8, core: 2. Of those that a mesh axis runs over, the one named last changes fastest.
Arguments:
- out_grad: bfloat16 [524288, 512], P(('clique', 'copy')), may hold values from -6 to 6
- pre_act: bfloat16 [524288, 512], P(('clique', 'copy')), may hold values from -6 to 6
- batch_count: int32 [256], P(('clique', 'copy')), may hold values from 1024 to 2048, as said below
- layer_two: bfloat16 [512, 512], replicated, may hold values from -0.25 to 0.25
- hot_slots: int32 [524288, 10], P(('clique', 'copy')), may hold values from 0 to 4095
- cold_index: int32 [524288, 15], P(('clique', 'copy')), may hold values from 0 to 2047
- hot_feats: bfloat16 [4096, 768], P('clique'), may hold values from -6 to 6
- cold_feats: bfloat16 [524288, 768], P(('clique', 'copy')), may hold values from -6 to 6
Outputs:
- grad_one: float32 [768, 512], replicated
- grad_two: float32 [512, 512], replicated
Inputs may be any that keep to these rules, and one draw needn't show every extreme that they name: `batch_count`: some device has all 2048 rows live in every draw.
All inputs are finite; a program needn't handle non-finite values.
Results may differ from a plain program's by a relative error of at most 0.015.
Values may be sent and summed in bfloat16 or wider, within the bound.
A program may use at most 128 MiB of HBM per device.

v0:
```python
import jax
import jax.numpy as jnp
from jax import lax
from jax.sharding import PartitionSpec as P


def table_sums(index_cols, row_grad, table_rows, fanout):
    block = min(512, table_rows)
    blocks = table_rows // block
    offsets = jnp.arange(block, dtype=jnp.int32)

    def one_block(start):
        wanted = start + offsets
        counts = jnp.zeros((block, index_cols.shape[0]), jnp.float32)
        for column in range(index_cols.shape[1]):
            counts = counts + (index_cols[:, column][None, :] == wanted[:, None]).astype(
                jnp.float32
            )
        summed = jnp.dot(counts.astype(jnp.bfloat16), row_grad, preferred_element_type=jnp.float32)
        return (summed * (1.0 / fanout)).astype(jnp.bfloat16)

    starts = jnp.arange(blocks, dtype=jnp.int32) * block
    parts = lax.map(one_block, starts)
    return parts.reshape(table_rows, row_grad.shape[1])


def on_device(
    out_grad, pre_act, batch_count, layer_two, hot_slots, cold_index, hot_feats, cold_feats
):
    rows = out_grad.shape[0]
    hot_local = hot_feats.shape[0]
    hot_total = hot_local * lax.axis_size("clique")
    k_hot = hot_slots.shape[1]
    k_cold = cold_index.shape[1]
    fanout = k_hot + k_cold
    cold_rows = cold_feats.shape[0]
    live = (jnp.arange(rows, dtype=jnp.int32) < batch_count[0])[:, None]
    masked = jnp.where(live, out_grad, jnp.zeros_like(out_grad))
    activ = jnp.maximum(pre_act, jnp.zeros_like(pre_act))
    grad_two = jnp.dot(activ.T, masked, preferred_element_type=jnp.float32)
    back = jnp.dot(masked, layer_two.T, preferred_element_type=jnp.float32)
    row_grad = jnp.where(pre_act > 0, back, jnp.zeros_like(back)).astype(jnp.bfloat16)
    hot_part = table_sums(hot_slots, row_grad, hot_total, fanout)
    summed = lax.psum(hot_part, "clique").astype(jnp.float32)
    owned = lax.dynamic_slice_in_dim(summed, lax.axis_index("clique") * hot_local, hot_local, 0)
    cold_part = table_sums(cold_index, row_grad, cold_rows, fanout)
    grad_one = jnp.dot(cold_feats.T, cold_part, preferred_element_type=jnp.float32)
    grad_one = grad_one + jnp.dot(
        hot_feats.T, owned.astype(jnp.bfloat16), preferred_element_type=jnp.float32
    )
    total_one, total_two = lax.psum((grad_one, grad_two), ("clique", "copy"))
    return (total_one, total_two)


def solution(mesh):
    placed = (
        P(("clique", "copy"), None),
        P(("clique", "copy"), None),
        P(("clique", "copy")),
        P(),
        P(("clique", "copy"), None),
        P(("clique", "copy"), None),
        P("clique", None),
        P(("clique", "copy"), None),
    )
    return jax.shard_map(
        on_device, mesh=mesh, in_specs=placed, out_specs=(P(), P()), check_vma=False
    )
```

profile of v0, /device:TPU:2, one launch (start us, length us, event | category | flops | bytes accessed | tf_op | source)
XLA Modules:
  0.0 475.0 jit_solution(12058573302038147682)
XLA Ops:
  8.1 5.2 %select_convert_fusion = bf16[2048,512]{1,0:T(8,128)(2,1)} fusion(bf16[2048,512]{1,0:T(8,128)(2,1)} %param.13, bf16[512,512]{1,0:T(8,128)(2,1)} %param.15, bf16[2048,512]{1,0:T(8,128)(2,1)} %param.12, pred[2048]{0:T(1024)(128)(4,1)S(1)} %iota_compare_fusion), kind=kOutput, calls=%fused_computation.43 | convolution fusion | flops 1077936128 | bytes 6817792 | tf_op jit(solution)/shard_map/dot_general | solution.py:41
  13.2 63.4 %while.23 = (s32[]{:T(128)}, bf16[8,512,512]{2,1,0:T(8,128)(2,1)}, s32[2048,10]{0,1:T(8,128)S(1)}, s32[8]{0:T(128)S(1)}, bf16[2048,512]{1,0:T(8,128)(2,1)}, /*index=5*/s32[]{:T(128)}) while((s32[]{:T(128)}, bf16[8,512,512]{2,1,0:T(8,128)(2,1)}, s32[2048,10]{0,1:T(8,128)S(1)}, s32[8]{0:T(128)S(1)}, bf16[2048,512]{1,0:T(8,128)(2,1)}, ...), condition=%wide.region_3.4_spmd.clone, body=%wide.region_2.3_spmd.clone.sunk | while | flops 1105723904 | bytes 2871893 | solution.py:23
  13.3 0.6 dynamic_slice.22
  14.6 6.6 %fusion.68 = bf16[8,512,512]{2,1,0:T(8,128)(2,1)} fusion(bf16[8,512,512]{2,1,0:T(8,128)(2,1)} %get-tuple-element.278, s32[]{:T(128)} %get-tuple-element.277, bf16[2048,512]{1,0:T(8,128)(2,1)} %get-tuple-element.287, s32[2048]{0:T(1024)S(1)} %bitcast.126, s32[2048]{0:T(1024)S(1)} %bitcast.127, s32[2048]{0:T(1024)S(1)} %bitcast.128, ...), kind=kOutput, calls=%fused_computation.41.clone.1 | convolution fusion | flops 1105723392 | bytes 2705920 | tf_op jit(solution)/shard_map/while/body/eval_jaxpr/dot_general | solution.py:19
  22.5 6.6 %fusion.68 = bf16[8,512,512]{2,1,0:T(8,128)(2,1)} fusion(bf16[8,512,512]{2,1,0:T(8,128)(2,1)} %get-tuple-element.278, s32[]{:T(128)} %get-tuple-element.277, bf16[2048,512]{1,0:T(8,128)(2,1)} %get-tuple-element.287, s32[2048]{0:T(1024)S(1)} %bitcast.126, s32[2048]{0:T(1024)S(1)} %bitcast.127, s32[2048]{0:T(1024)S(1)} %bitcast.128, ...), kind=kOutput, calls=%fused_computation.41.clone.1 | convolution fusion | flops 1105723392 | bytes 2705920 | tf_op jit(solution)/shard_map/while/body/eval_jaxpr/dot_general | solution.py:19
  29.2 0.6 dynamic_slice.22
  30.4 6.6 %fusion.68 = bf16[8,512,512]{2,1,0:T(8,128)(2,1)} fusion(bf16[8,512,512]{2,1,0:T(8,128)(2,1)} %get-tuple-element.278, s32[]{:T(128)} %get-tuple-element.277, bf16[2048,512]{1,0:T(8,128)(2,1)} %get-tuple-element.287, s32[2048]{0:T(1024)S(1)} %bitcast.126, s32[2048]{0:T(1024)S(1)} %bitcast.127, s32[2048]{0:T(1024)S(1)} %bitcast.128, ...), kind=kOutput, calls=%fused_computation.41.clone.1 | convolution fusion | flops 1105723392 | bytes 2705920 | tf_op jit(solution)/shard_map/while/body/eval_jaxpr/dot_general | solution.py:19
  38.4 6.6 %fusion.68 = bf16[8,512,512]{2,1,0:T(8,128)(2,1)} fusion(bf16[8,512,512]{2,1,0:T(8,128)(2,1)} %get-tuple-element.278, s32[]{:T(128)} %get-tuple-element.277, bf16[2048,512]{1,0:T(8,128)(2,1)} %get-tuple-element.287, s32[2048]{0:T(1024)S(1)} %bitcast.126, s32[2048]{0:T(1024)S(1)} %bitcast.127, s32[2048]{0:T(1024)S(1)} %bitcast.128, ...), kind=kOutput, calls=%fused_computation.41.clone.1 | convolution fusion | flops 1105723392 | bytes 2705920 | tf_op jit(solution)/shard_map/while/body/eval_jaxpr/dot_general | solution.py:19
  46.3 6.6 %fusion.68 = bf16[8,512,512]{2,1,0:T(8,128)(2,1)} fusion(bf16[8,512,512]{2,1,0:T(8,128)(2,1)} %get-tuple-element.278, s32[]{:T(128)} %get-tuple-element.277, bf16[2048,512]{1,0:T(8,128)(2,1)} %get-tuple-element.287, s32[2048]{0:T(1024)S(1)} %bitcast.126, s32[2048]{0:T(1024)S(1)} %bitcast.127, s32[2048]{0:T(1024)S(1)} %bitcast.128, ...), kind=kOutput, calls=%fused_computation.41.clone.1 | convolution fusion | flops 1105723392 | bytes 2705920 | tf_op jit(solution)/shard_map/while/body/eval_jaxpr/dot_general | solution.py:19
  54.2 6.6 %fusion.68 = bf16[8,512,512]{2,1,0:T(8,128)(2,1)} fusion(bf16[8,512,512]{2,1,0:T(8,128)(2,1)} %get-tuple-element.278, s32[]{:T(128)} %get-tuple-element.277, bf16[2048,512]{1,0:T(8,128)(2,1)} %get-tuple-element.287, s32[2048]{0:T(1024)S(1)} %bitcast.126, s32[2048]{0:T(1024)S(1)} %bitcast.127, s32[2048]{0:T(1024)S(1)} %bitcast.128, ...), kind=kOutput, calls=%fused_computation.41.clone.1 | convolution fusion | flops 1105723392 | bytes 2705920 | tf_op jit(solution)/shard_map/while/body/eval_jaxpr/dot_general | solution.py:19
  62.1 6.6 %fusion.68 = bf16[8,512,512]{2,1,0:T(8,128)(2,1)} fusion(bf16[8,512,512]{2,1,0:T(8,128)(2,1)} %get-tuple-element.278, s32[]{:T(128)} %get-tuple-element.277, bf16[2048,512]{1,0:T(8,128)(2,1)} %get-tuple-element.287, s32[2048]{0:T(1024)S(1)} %bitcast.126, s32[2048]{0:T(1024)S(1)} %bitcast.127, s32[2048]{0:T(1024)S(1)} %bitcast.128, ...), kind=kOutput, calls=%fused_computation.41.clone.1 | convolution fusion | flops 1105723392 | bytes 2705920 | tf_op jit(solution)/shard_map/while/body/eval_jaxpr/dot_general | solution.py:19
  70.1 6.6 %fusion.68 = bf16[8,512,512]{2,1,0:T(8,128)(2,1)} fusion(bf16[8,512,512]{2,1,0:T(8,128)(2,1)} %get-tuple-element.278, s32[]{:T(128)} %get-tuple-element.277, bf16[2048,512]{1,0:T(8,128)(2,1)} %get-tuple-element.287, s32[2048]{0:T(1024)S(1)} %bitcast.126, s32[2048]{0:T(1024)S(1)} %bitcast.127, s32[2048]{0:T(1024)S(1)} %bitcast.128, ...), kind=kOutput, calls=%fused_computation.41.clone.1 | convolution fusion | flops 1105723392 | bytes 2705920 | tf_op jit(solution)/shard_map/while/body/eval_jaxpr/dot_general | solution.py:19
  77.0 4.6 fusion.41
  81.5 39.8 %while.22 = (s32[]{:T(128)}, bf16[4,512,512]{2,1,0:T(8,128)(2,1)}, s32[2048,15]{0,1:T(8,128)S(1)}, s32[4]{0:T(128)S(1)}, bf16[2048,512]{1,0:T(8,128)(2,1)}, /*index=5*/s32[]{:T(128)}) while((s32[]{:T(128)}, bf16[4,512,512]{2,1,0:T(8,128)(2,1)}, s32[2048,15]{0,1:T(8,128)S(1)}, s32[4]{0:T(128)S(1)}, bf16[2048,512]{1,0:T(8,128)(2,1)}, ...), condition=%wide.region_1.2_spmd.clone, body=%wide.region_0.1_spmd.clone.sunk | while | flops 1121452544 | bytes 2994773 | solution.py:23
  82.9 8.6 %fusion.65 = bf16[4,512,512]{2,1,0:T(8,128)(2,1)} fusion(bf16[4,512,512]{2,1,0:T(8,128)(2,1)} %get-tuple-element.260, s32[]{:T(128)} %get-tuple-element.259, bf16[2048,512]{1,0:T(8,128)(2,1)} %get-tuple-element.269, s32[2048]{0:T(1024)S(1)} %bitcast.111, s32[2048]{0:T(1024)S(1)} %bitcast.112, s32[2048]{0:T(1024)S(1)} %bitcast.113, ...), kind=kOutput, calls=%fused_computation.23.clone.1 | convolution fusion | flops 1121452032 | bytes 2746880 | tf_op jit(solution)/shard_map/while/body/eval_jaxpr/dot_general | solution.py:19
  92.9 8.6 %fusion.65 = bf16[4,512,512]{2,1,0:T(8,128)(2,1)} fusion(bf16[4,512,512]{2,1,0:T(8,128)(2,1)} %get-tuple-element.260, s32[]{:T(128)} %get-tuple-element.259, bf16[2048,512]{1,0:T(8,128)(2,1)} %get-tuple-element.269, s32[2048]{0:T(1024)S(1)} %bitcast.111, s32[2048]{0:T(1024)S(1)} %bitcast.112, s32[2048]{0:T(1024)S(1)} %bitcast.113, ...), kind=kOutput, calls=%fused_computation.23.clone.1 | convolution fusion | flops 1121452032 | bytes 2746880 | tf_op jit(solution)/shard_map/while/body/eval_jaxpr/dot_general | solution.py:19
  102.8 8.6 %fusion.65 = bf16[4,512,512]{2,1,0:T(8,128)(2,1)} fusion(bf16[4,512,512]{2,1,0:T(8,128)(2,1)} %get-tuple-element.260, s32[]{:T(128)} %get-tuple-element.259, bf16[2048,512]{1,0:T(8,128)(2,1)} %get-tuple-element.269, s32[2048]{0:T(1024)S(1)} %bitcast.111, s32[2048]{0:T(1024)S(1)} %bitcast.112, s32[2048]{0:T(1024)S(1)} %bitcast.113, ...), kind=kOutput, calls=%fused_computation.23.clone.1 | convolution fusion | flops 1121452032 | bytes 2746880 | tf_op jit(solution)/shard_map/while/body/eval_jaxpr/dot_general | solution.py:19
  112.8 8.6 %fusion.65 = bf16[4,512,512]{2,1,0:T(8,128)(2,1)} fusion(bf16[4,512,512]{2,1,0:T(8,128)(2,1)} %get-tuple-element.260, s32[]{:T(128)} %get-tuple-element.259, bf16[2048,512]{1,0:T(8,128)(2,1)} %get-tuple-element.269, s32[2048]{0:T(1024)S(1)} %bitcast.111, s32[2048]{0:T(1024)S(1)} %bitcast.112, s32[2048]{0:T(1024)S(1)} %bitcast.113, ...), kind=kOutput, calls=%fused_computation.23.clone.1 | convolution fusion | flops 1121452032 | bytes 2746880 | tf_op jit(solution)/shard_map/while/body/eval_jaxpr/dot_general | solution.py:19
  121.4 4.6 fusion.50
  126.0 66.5 %all-reduce.4.cloned.1.call-done = bf16[4096,512]{1,0:T(8,128)(2,1)} async-done(((bf16[4096,512]{1,0:T(8,128)(2,1)}), bf16[4096,512]{1,0:T(8,128)(2,1)}) %all-reduce.4.cloned.1.call-update) | async-done | bytes 4194320 | tf_op jit(solution)/shard_map/psum | solution.py:44
  192.5 3.6 add_bitcast_fusion
  196.0 266.8 %all-reduce.6.cloned.1.call-done = (f32[768,512]{0,1:T(8,128)}, f32[512,512]{1,0:T(8,128)}) async-done(((f32[768,512]{0,1:T(8,128)}, f32[512,512]{1,0:T(8,128)}), (f32[768,512]{0,1:T(8,128)}, f32[512,512]{1,0:T(8,128)})) %all-reduce.6.cloned.1.call-update) | async-done | bytes 2621456 | tf_op jit(solution)/shard_map/psum | solution.py:51
  462.9 3.0 copy.10
  465.9 2.3 copy.30
  (49 shorter events, 14.9 us)
Async XLA Ops:
  7.2 114.2 %copy-start = (bf16[2048,768]{1,0:T(8,128)(2,1)S(1)}, bf16[2048,768]{1,0:T(8,128)(2,1)}, u32[]{:S(2)}) copy-start(bf16[2048,768]{1,0:T(8,128)(2,1)} %param.19) | copy-start | bytes 9437188
  7.2 185.3 %all-reduce.4.cloned.1.call-start = ((), (), s32[]{:S(2)}) async-start(), calls=%async_computation | async-start | bytes 8388608 | tf_op jit(solution)/shard_map/psum | solution.py:44
  8.1 5.2 %copy-start.2 = (s32[2048,10]{0,1:T(8,128)S(1)}, s32[2048,10]{0,1:T(8,128)}, u32[]{:S(2)}) copy-start(s32[2048,10]{0,1:T(8,128)} %param.16) | copy-start | bytes 245764
  76.7 4.8 %copy-start.1 = (s32[2048,15]{0,1:T(8,128)S(1)}, s32[2048,15]{0,1:T(8,128)}, u32[]{:S(2)}) copy-start(s32[2048,15]{0,1:T(8,128)} %param.17) | copy-start | bytes 368644
  76.7 386.1 %all-reduce.6.cloned.1.call-start = ((), (), s32[]{:S(2)}) async-start(), calls=%async_computation.1 | async-start | bytes 5242880 | tf_op jit(solution)/shard_map/psum | solution.py:51
Sparse Core Ops, SparseCore 0:
  76.8 115.5 all-reduce.3
  198.6 264.2 all-reduce.5
where the time goes:
time: 476 us; the launch traced here: 475 us
  waiting for transfers between devices  333 us (70%)
  matrix products  105 us (22%)
  between operations  14.9 us (3%)
  local copies, waits for them, and re-layouts  13.6 us (3%)
  other arithmetic  7.56 us (2%)
    psum x1, waiting for transfers between devices, on_device(): total_one, total_two = lax.psum((grad_one, grad_two), ('clique', 'copy'))  267 us
    dot_general x12, matrix products, one_block(): jnp.dot(counts.astype(jnp.bfloat16), row_grad, preferred_element_type=jnp...  87.3 us
    psum x1, waiting for transfers between devices, on_device(): summed = lax.psum(hot_part, 'clique').astype(jnp.float32)  66.5 us
  transfers between devices with their start and end apart: 2, of which 2 were waited for; matrix products, arithmetic and copies ran while one was open for 10% of the time, Pallas kernels for 0%

commit v1 on v0

--- a/solution.py
+++ b/solution.py
@@ -48,7 +48,7 @@
     grad_one = grad_one + jnp.dot(
         hot_feats.T, owned.astype(jnp.bfloat16), preferred_element_type=jnp.float32
     )
-    total_one, total_two = lax.psum((grad_one, grad_two), ("clique", "copy"))
+    total_one, total_two = lax.psum(lax.psum((grad_one, grad_two), "clique"), "copy")
     return (total_one, total_two)
 
 

time: 476 us -> 547 us (1.15)
  waiting for transfers between devices: 333 us -> 403 us
    psum x1 -> x2, waiting for transfers between devices: 267 us -> 337 us  [the longest x1 237 us: on_device(): lax.psum(lax.psum((grad_one, grad_two), 'clique'), 'copy')]
  transfers between devices with their start and end apart: 2 -> 3, of which waited for: 2 -> 3; matrix products, arithmetic and copies ran while one was open for 10% -> 9% of each run, Pallas kernels for 0% -> 0%
where the time goes in v1:
time: 547 us; the launch traced here: 545 us
  waiting for transfers between devices  403 us (74%)
  matrix products  105 us (19%)
  between operations  14.6 us (3%)
  local copies, waits for them, and re-layouts  13.7 us (3%)
  other arithmetic  7.46 us (1%)
    psum x1, waiting for transfers between devices, on_device(): lax.psum(lax.psum((grad_one, grad_two), 'clique'), 'copy')  237 us
    psum x1, waiting for transfers between devices, on_device(): lax.psum((grad_one, grad_two), 'clique')  99.7 us
    dot_general x12, matrix products, one_block(): jnp.dot(counts.astype(jnp.bfloat16), row_grad, preferred_element_type=jnp...  87.3 us
    psum x1, waiting for transfers between devices, on_device(): summed = lax.psum(hot_part, 'clique').astype(jnp.float32)  66.6 us
  transfers between devices with their start and end apart: 3, of which 3 were waited for; matrix products, arithmetic and copies ran while one was open for 9% of the time, Pallas kernels for 0%

profile of v1, /device:TPU:2, one launch (start us, length us, event | category | flops | bytes accessed | tf_op | source)
XLA Modules:
  0.0 544.8 jit_solution(13814576440545793151)
XLA Ops:
  8.1 5.2 select_convert_fusion
  13.3 63.5 %while.23 = (s32[]{:T(128)}, bf16[8,512,512]{2,1,0:T(8,128)(2,1)}, s32[2048,10]{0,1:T(8,128)S(1)}, s32[8]{0:T(128)S(1)}, bf16[2048,512]{1,0:T(8,128)(2,1)}, /*index=5*/s32[]{:T(128)}) while((s32[]{:T(128)}, bf16[8,512,512]{2,1,0:T(8,128)(2,1)}, s32[2048,10]{0,1:T(8,128)S(1)}, s32[8]{0:T(128)S(1)}, bf16[2048,512]{1,0:T(8,128)(2,1)}, ...), condition=%wide.region_3.4_spmd.clone, body=%wide.region_2.3_spmd.clone.sunk | while | flops 1105723904 | bytes 2871893 | solution.py:23
  13.3 0.7 dynamic_slice.22
  14.6 6.6 %fusion.68 = bf16[8,512,512]{2,1,0:T(8,128)(2,1)} fusion(bf16[8,512,512]{2,1,0:T(8,128)(2,1)} %get-tuple-element.280, s32[]{:T(128)} %get-tuple-element.279, bf16[2048,512]{1,0:T(8,128)(2,1)} %get-tuple-element.289, s32[2048]{0:T(1024)S(1)} %bitcast.126, s32[2048]{0:T(1024)S(1)} %bitcast.127, s32[2048]{0:T(1024)S(1)} %bitcast.128, ...), kind=kOutput, calls=%fused_computation.41.clone.1 | convolution fusion | flops 1105723392 | bytes 2705920 | tf_op jit(solution)/shard_map/while/body/eval_jaxpr/dot_general | solution.py:19
  22.5 6.6 %fusion.68 = bf16[8,512,512]{2,1,0:T(8,128)(2,1)} fusion(bf16[8,512,512]{2,1,0:T(8,128)(2,1)} %get-tuple-element.280, s32[]{:T(128)} %get-tuple-element.279, bf16[2048,512]{1,0:T(8,128)(2,1)} %get-tuple-element.289, s32[2048]{0:T(1024)S(1)} %bitcast.126, s32[2048]{0:T(1024)S(1)} %bitcast.127, s32[2048]{0:T(1024)S(1)} %bitcast.128, ...), kind=kOutput, calls=%fused_computation.41.clone.1 | convolution fusion | flops 1105723392 | bytes 2705920 | tf_op jit(solution)/shard_map/while/body/eval_jaxpr/dot_general | solution.py:19
  30.5 6.6 %fusion.68 = bf16[8,512,512]{2,1,0:T(8,128)(2,1)} fusion(bf16[8,512,512]{2,1,0:T(8,128)(2,1)} %get-tuple-element.280, s32[]{:T(128)} %get-tuple-element.279, bf16[2048,512]{1,0:T(8,128)(2,1)} %get-tuple-element.289, s32[2048]{0:T(1024)S(1)} %bitcast.126, s32[2048]{0:T(1024)S(1)} %bitcast.127, s32[2048]{0:T(1024)S(1)} %bitcast.128, ...), kind=kOutput, calls=%fused_computation.41.clone.1 | convolution fusion | flops 1105723392 | bytes 2705920 | tf_op jit(solution)/shard_map/while/body/eval_jaxpr/dot_general | solution.py:19
  38.4 6.6 %fusion.68 = bf16[8,512,512]{2,1,0:T(8,128)(2,1)} fusion(bf16[8,512,512]{2,1,0:T(8,128)(2,1)} %get-tuple-element.280, s32[]{:T(128)} %get-tuple-element.279, bf16[2048,512]{1,0:T(8,128)(2,1)} %get-tuple-element.289, s32[2048]{0:T(1024)S(1)} %bitcast.126, s32[2048]{0:T(1024)S(1)} %bitcast.127, s32[2048]{0:T(1024)S(1)} %bitcast.128, ...), kind=kOutput, calls=%fused_computation.41.clone.1 | convolution fusion | flops 1105723392 | bytes 2705920 | tf_op jit(solution)/shard_map/while/body/eval_jaxpr/dot_general | solution.py:19
  46.3 6.6 %fusion.68 = bf16[8,512,512]{2,1,0:T(8,128)(2,1)} fusion(bf16[8,512,512]{2,1,0:T(8,128)(2,1)} %get-tuple-element.280, s32[]{:T(128)} %get-tuple-element.279, bf16[2048,512]{1,0:T(8,128)(2,1)} %get-tuple-element.289, s32[2048]{0:T(1024)S(1)} %bitcast.126, s32[2048]{0:T(1024)S(1)} %bitcast.127, s32[2048]{0:T(1024)S(1)} %bitcast.128, ...), kind=kOutput, calls=%fused_computation.41.clone.1 | convolution fusion | flops 1105723392 | bytes 2705920 | tf_op jit(solution)/shard_map/while/body/eval_jaxpr/dot_general | solution.py:19
  54.3 6.6 %fusion.68 = bf16[8,512,512]{2,1,0:T(8,128)(2,1)} fusion(bf16[8,512,512]{2,1,0:T(8,128)(2,1)} %get-tuple-element.280, s32[]{:T(128)} %get-tuple-element.279, bf16[2048,512]{1,0:T(8,128)(2,1)} %get-tuple-element.289, s32[2048]{0:T(1024)S(1)} %bitcast.126, s32[2048]{0:T(1024)S(1)} %bitcast.127, s32[2048]{0:T(1024)S(1)} %bitcast.128, ...), kind=kOutput, calls=%fused_computation.41.clone.1 | convolution fusion | flops 1105723392 | bytes 2705920 | tf_op jit(solution)/shard_map/while/body/eval_jaxpr/dot_general | solution.py:19
  62.2 6.6 %fusion.68 = bf16[8,512,512]{2,1,0:T(8,128)(2,1)} fusion(bf16[8,512,512]{2,1,0:T(8,128)(2,1)} %get-tuple-element.280, s32[]{:T(128)} %get-tuple-element.279, bf16[2048,512]{1,0:T(8,128)(2,1)} %get-tuple-element.289, s32[2048]{0:T(1024)S(1)} %bitcast.126, s32[2048]{0:T(1024)S(1)} %bitcast.127, s32[2048]{0:T(1024)S(1)} %bitcast.128, ...), kind=kOutput, calls=%fused_computation.41.clone.1 | convolution fusion | flops 1105723392 | bytes 2705920 | tf_op jit(solution)/shard_map/while/body/eval_jaxpr/dot_general | solution.py:19
  70.1 6.6 %fusion.68 = bf16[8,512,512]{2,1,0:T(8,128)(2,1)} fusion(bf16[8,512,512]{2,1,0:T(8,128)(2,1)} %get-tuple-element.280, s32[]{:T(128)} %get-tuple-element.279, bf16[2048,512]{1,0:T(8,128)(2,1)} %get-tuple-element.289, s32[2048]{0:T(1024)S(1)} %bitcast.126, s32[2048]{0:T(1024)S(1)} %bitcast.127, s32[2048]{0:T(1024)S(1)} %bitcast.128, ...), kind=kOutput, calls=%fused_computation.41.clone.1 | convolution fusion | flops 1105723392 | bytes 2705920 | tf_op jit(solution)/shard_map/while/body/eval_jaxpr/dot_general | solution.py:19
  77.1 4.5 fusion.41
  81.6 39.7 %while.22 = (s32[]{:T(128)}, bf16[4,512,512]{2,1,0:T(8,128)(2,1)}, s32[2048,15]{0,1:T(8,128)S(1)}, s32[4]{0:T(128)S(1)}, bf16[2048,512]{1,0:T(8,128)(2,1)}, /*index=5*/s32[]{:T(128)}) while((s32[]{:T(128)}, bf16[4,512,512]{2,1,0:T(8,128)(2,1)}, s32[2048,15]{0,1:T(8,128)S(1)}, s32[4]{0:T(128)S(1)}, bf16[2048,512]{1,0:T(8,128)(2,1)}, ...), condition=%wide.region_1.2_spmd.clone, body=%wide.region_0.1_spmd.clone.sunk | while | flops 1121452544 | bytes 2994773 | solution.py:23
  82.9 8.6 %fusion.65 = bf16[4,512,512]{2,1,0:T(8,128)(2,1)} fusion(bf16[4,512,512]{2,1,0:T(8,128)(2,1)} %get-tuple-element.262, s32[]{:T(128)} %get-tuple-element.261, bf16[2048,512]{1,0:T(8,128)(2,1)} %get-tuple-element.271, s32[2048]{0:T(1024)S(1)} %bitcast.111, s32[2048]{0:T(1024)S(1)} %bitcast.112, s32[2048]{0:T(1024)S(1)} %bitcast.113, ...), kind=kOutput, calls=%fused_computation.23.clone.1 | convolution fusion | flops 1121452032 | bytes 2746880 | tf_op jit(solution)/shard_map/while/body/eval_jaxpr/dot_general | solution.py:19
  92.8 8.6 %fusion.65 = bf16[4,512,512]{2,1,0:T(8,128)(2,1)} fusion(bf16[4,512,512]{2,1,0:T(8,128)(2,1)} %get-tuple-element.262, s32[]{:T(128)} %get-tuple-element.261, bf16[2048,512]{1,0:T(8,128)(2,1)} %get-tuple-element.271, s32[2048]{0:T(1024)S(1)} %bitcast.111, s32[2048]{0:T(1024)S(1)} %bitcast.112, s32[2048]{0:T(1024)S(1)} %bitcast.113, ...), kind=kOutput, calls=%fused_computation.23.clone.1 | convolution fusion | flops 1121452032 | bytes 2746880 | tf_op jit(solution)/shard_map/while/body/eval_jaxpr/dot_general | solution.py:19
  102.8 8.6 %fusion.65 = bf16[4,512,512]{2,1,0:T(8,128)(2,1)} fusion(bf16[4,512,512]{2,1,0:T(8,128)(2,1)} %get-tuple-element.262, s32[]{:T(128)} %get-tuple-element.261, bf16[2048,512]{1,0:T(8,128)(2,1)} %get-tuple-element.271, s32[2048]{0:T(1024)S(1)} %bitcast.111, s32[2048]{0:T(1024)S(1)} %bitcast.112, s32[2048]{0:T(1024)S(1)} %bitcast.113, ...), kind=kOutput, calls=%fused_computation.23.clone.1 | convolution fusion | flops 1121452032 | bytes 2746880 | tf_op jit(solution)/shard_map/while/body/eval_jaxpr/dot_general | solution.py:19
  112.7 8.6 %fusion.65 = bf16[4,512,512]{2,1,0:T(8,128)(2,1)} fusion(bf16[4,512,512]{2,1,0:T(8,128)(2,1)} %get-tuple-element.262, s32[]{:T(128)} %get-tuple-element.261, bf16[2048,512]{1,0:T(8,128)(2,1)} %get-tuple-element.271, s32[2048]{0:T(1024)S(1)} %bitcast.111, s32[2048]{0:T(1024)S(1)} %bitcast.112, s32[2048]{0:T(1024)S(1)} %bitcast.113, ...), kind=kOutput, calls=%fused_computation.23.clone.1 | convolution fusion | flops 1121452032 | bytes 2746880 | tf_op jit(solution)/shard_map/while/body/eval_jaxpr/dot_general | solution.py:19
  121.3 4.6 fusion.50
  125.9 66.6 %all-reduce.6.cloned.1.call-done = bf16[4096,512]{1,0:T(8,128)(2,1)} async-done(((bf16[4096,512]{1,0:T(8,128)(2,1)}), bf16[4096,512]{1,0:T(8,128)(2,1)}) %all-reduce.6.cloned.1.call-update) | async-done | bytes 4194320 | tf_op jit(solution)/shard_map/psum | solution.py:44
  192.6 3.6 add_bitcast_fusion
  196.2 99.7 %all-reduce.10.cloned.1.call-done = (f32[768,512]{0,1:T(8,128)}, f32[512,512]{1,0:T(8,128)}) async-done(((f32[768,512]{0,1:T(8,128)}, f32[512,512]{1,0:T(8,128)}), (f32[768,512]{0,1:T(8,128)}, f32[512,512]{1,0:T(8,128)})) %all-reduce.10.cloned.1.call-update) | async-done | bytes 2621456 | tf_op jit(solution)/shard_map/psum | solution.py:51
  296.0 237.0 %all-reduce.8.cloned.1.call-done = (f32[768,512]{0,1:T(8,128)}, f32[512,512]{1,0:T(8,128)}) async-done(((f32[768,512]{0,1:T(8,128)}, f32[512,512]{1,0:T(8,128)}), (f32[768,512]{0,1:T(8,128)}, f32[512,512]{1,0:T(8,128)})) %all-reduce.8.cloned.1.call-update) | async-done | bytes 2621456 | tf_op jit(solution)/shard_map/psum | solution.py:51
  533.0 3.0 copy.10
  536.0 2.3 copy.32
  (52 shorter events, 15.5 us)
Async XLA Ops:
  7.2 114.2 %copy-start = (bf16[2048,768]{1,0:T(8,128)(2,1)S(1)}, bf16[2048,768]{1,0:T(8,128)(2,1)}, u32[]{:S(2)}) copy-start(bf16[2048,768]{1,0:T(8,128)(2,1)} %param.19) | copy-start | bytes 9437188
  7.2 185.4 %all-reduce.6.cloned.1.call-start = ((), (), s32[]{:S(2)}) async-start(), calls=%async_computation | async-start | bytes 8388608 | tf_op jit(solution)/shard_map/psum | solution.py:44
  8.1 5.2 copy-start.2
  76.8 4.8 copy-start.1
  76.8 219.1 %all-reduce.10.cloned.1.call-start = ((), (), s32[]{:S(2)}) async-start(), calls=%async_computation.2 | async-start | bytes 5242880 | tf_op jit(solution)/shard_map/psum | solution.py:51
  196.2 336.8 %all-reduce.8.cloned.1.call-start = ((), (), s32[]{:S(2)}) async-start(), calls=%async_computation.1 | async-start | bytes 5242880 | tf_op jit(solution)/shard_map/psum | solution.py:51
Sparse Core Ops, SparseCore 0:
  76.9 115.6 all-reduce.5
  196.3 99.6 all-reduce.9
  298.6 234.3 all-reduce.7
